TPU v7x, 256 devices: a whole 4x4x8 slice. The times are simulated.
256 devices in a mesh: dp: 8 (over z), vocab: 32 (over y, x, core).
Axes of the slice: x: 4, y: 4, z: 8, core: 2. Of those that a mesh axis runs over, the one named last changes fastest.
Arguments:
- hidden: bfloat16 [5120, 4096], P(('dp', 'vocab')), may hold values from -192 to 192, as said below
- out_weight: bfloat16 [4096, 81920], P('dp', 'vocab'), may hold values from -0.09375 to 0.09375
- labels: int32 [5120], P('dp'), may hold values from 0 to 81919
- text_mask: int32 [5120], P('dp'), may hold values from 0 to 1, as said below
Outputs:
- token_loss: float32 [5120], P('dp')
- mean_loss: float32 [], replicated
Inputs may be any that keep to these rules, and one draw needn't show every extreme that they name: The hidden states are of moderate size in most rows, possibly larger in a few. `text_mask`: vision and text tokens come in runs of 16 aligned tokens.
All inputs are finite; a program needn't handle non-finite values.
Results may differ from a plain program's by a relative error of at most 0.0003.
Values may be sent and summed in bfloat16 or wider, within the bound.
A program may use at most 128 MiB of HBM per device.

v0:
```python
import jax
import jax.numpy as jnp
from jax import lax
from jax.sharding import PartitionSpec as P


def from_everyone(x, axis):
    devices = lax.axis_size(axis)
    return lax.all_to_all(jnp.broadcast_to(x[None], (devices, *x.shape)), axis, 0, 0, tiled=True)


def collected_together(x, axis):
    leaves = jax.tree.leaves(x)
    order = sorted(range(len(leaves)), key=lambda k: -leaves[k].size)
    width = (1, *leaves[order[0]].shape)[-1]
    lines = [
        jnp.pad(leaves[k].reshape(-1), (0, -leaves[k].size % width)).reshape(-1, width)
        for k in order
    ]
    both, at, found = (from_everyone(jnp.concatenate(lines), axis), 0, {})
    for k, line in zip(order, lines):
        slab = both[:, at : at + len(line)].reshape(len(both), -1)
        found[k] = slab[:, : leaves[k].size].reshape(-1, *leaves[k].shape)
        at += len(line)
    numbers = iter(range(len(leaves)))
    return jax.tree.map(lambda _: found[next(numbers)], x)


def joined_by_halves(pieces, combine):
    while len(jax.tree.leaves(pieces)[0]) > 1:
        pieces = jax.vmap(combine)(
            *(jax.tree.map(lambda part: part[side::2], pieces) for side in (0, 1))
        )
    return jax.tree.map(lambda part: part[0], pieces)


def joined_all(x, axis, combine):
    pieces = collected_together(x, axis)
    return joined_by_halves(pieces, combine)


def over_copies(x, axis):
    return from_everyone(x, axis).sum(axis=0)


def packed_total(arrays, axis):
    line, at, done = (jnp.concatenate([a.reshape(-1) for a in arrays]), 0, [])
    so_far = over_copies(line, axis)
    for a in arrays:
        done.append(so_far[at : at + a.size].reshape(a.shape))
        at += a.size
    return tuple(done)


def shards(hidden, out_weight, labels, text_mask):
    gathered = lax.all_gather(hidden, "vocab", axis=0, tiled=True)
    width_here = out_weight.shape[1]
    first_column = lax.axis_index("vocab") * width_here
    weight_full = lax.all_gather(out_weight, "dp", axis=0, tiled=True)
    logits = jnp.dot(gathered, weight_full, preferred_element_type=jnp.float32)
    columns = jnp.arange(width_here, dtype=jnp.int32)
    local_targets = labels - first_column
    picked = jnp.sum(
        jnp.where(columns[None, :] == local_targets[:, None], logits, jnp.float32(0.0)), axis=1
    )
    local_top = jnp.max(logits, axis=1)
    weights_text = text_mask.astype(jnp.float32)
    local_total = jnp.sum(jnp.exp(logits - local_top[:, None]), axis=1)

    def combine(first, second):
        upper = jnp.maximum(first[0], second[0])
        summed = first[1] * jnp.exp(first[0] - upper) + second[1] * jnp.exp(second[0] - upper)
        return (upper, summed, first[2] + second[2])

    row_top, exp_total, label_logit = joined_all((local_top, local_total, picked), "vocab", combine)
    token_loss = weights_text * (row_top + jnp.log(exp_total) - label_logit)
    loss_sum, tally = packed_total((jnp.sum(token_loss), jnp.sum(weights_text)), "dp")
    mean_loss = loss_sum / jnp.maximum(tally, jnp.float32(1.0))
    return (token_loss, mean_loss)


def solution(mesh):
    in_specs = (P(("dp", "vocab"), None), P("dp", "vocab"), P("dp"), P("dp"))
    out_specs = (P("dp"), P())
    return jax.shard_map(shards, mesh=mesh, in_specs=in_specs, out_specs=out_specs, check_vma=False)
```

profile of v0, /device:TPU:1, one launch (start us, length us, event | category | flops | bytes accessed | tf_op | source)
XLA Modules:
  0.0 342.3 jit_solution(15762076118572349161)
XLA Ops:
  7.2 0.0 all-gather.6.cloned.1.call-start
  7.2 0.7 all-gather.6.cloned.1.call-update
  7.9 0.0 all-gather.4.cloned.1.call-start
  7.9 0.7 all-gather.4.cloned.1.call-update
  8.7 0.7 broadcast_subtract_fusion
  9.3 59.4 %all-gather.6.cloned.1.call-done = bf16[32,20,4096]{2,1,0:T(8,128)(2,1)} async-done(((bf16[1,20,4096]{2,1,0:T(8,128)(2,1)}), bf16[32,20,4096]{2,1,0:T(8,128)(2,1)}) %all-gather.6.cloned.1.call-update) | async-done | bytes 5242896 | tf_op jit(solution)/shard_map/all_gather | solution.py:56
  68.7 7.8 %reshape.54 = bf16[640,4096]{1,0:T(8,128)(2,1)} reshape(bf16[32,20,4096]{2,1,0:T(8,128)(2,1)} %all-gather.6.cloned.1.call-done) | data formatting | bytes 10485760
  76.5 204.4 %all-gather.4.cloned.1.call-done = bf16[4096,2560]{1,0:T(8,128)(2,1)} async-done(((bf16[512,2560]{1,0:T(8,128)(2,1)}), bf16[4096,2560]{1,0:T(8,128)(2,1)}) %all-gather.4.cloned.1.call-update) | async-done | bytes 20971536 | tf_op jit(solution)/shard_map/all_gather | solution.py:59
  280.9 18.6 %fusion.7 = (f32[640]{0:T(1024)S(1)}, f32[640,2560]{1,0:T(8,128)S(1)}) fusion(bf16[640,4096]{1,0:T(8,128)(2,1)} %reshape.54, bf16[4096,2560]{1,0:T(8,128)(2,1)} %all-gather.4.cloned.1.call-done), kind=kOutput, calls=%fused_computation.26 | convolution fusion | flops 13423410176 | bytes 32770560 | tf_op jit(solution)/shard_map/dot_general | solution.py:60
  299.5 0.0 copy-start
  299.5 1.7 exponential_reduce_fusion
  301.3 17.0 %all_to_all.11 = f32[32,3,640]{2,1,0:T(4,128)S(1)} all-to-all(f32[32,3,640]{2,1,0:T(4,128)S(1)} %broadcast_in_dim.9), channel_id=1, replica_groups=mesh['dp'=8,'vocab'=32] {'vocab'}, dimensions={0} | all-to-all | bytes 491520 | tf_op jit(solution)/shard_map/all_to_all | solution.py:9
  318.3 0.2 fusion.5
  319.3 0.0 copy-done
  319.3 1.3 fusion.4
  320.6 1.4 pad_maximum_fusion.1
  322.0 10.4 %all_to_all.12 = f32[8,1,2]{2,1,0:T(1,128)S(1)} all-to-all(f32[8,1,2]{2,1,0:T(1,128)S(1)} %broadcast_in_dim.10), channel_id=1, replica_groups=mesh['dp'=8,'vocab'=32] {'dp'}, dimensions={0} | all-to-all | bytes 128 | tf_op jit(solution)/shard_map/all_to_all | solution.py:9
  332.4 0.6 fusion.6
  (42 shorter events, 0.8 us)
Async XLA Ops:
  7.2 61.5 %all-gather.6.cloned.1.call-start = ((), (), s32[]{:S(2)}) async-start(), calls=%async_computation.3 | async-start | bytes 6488064 | tf_op jit(solution)/shard_map/all_gather | solution.py:56
  7.9 273.0 %all-gather.4.cloned.1.call-start = ((), (), s32[]{:S(2)}) async-start(), calls=%async_computation.2 | async-start | bytes 23592960 | tf_op jit(solution)/shard_map/all_gather | solution.py:59
  299.5 19.8 %copy-start = (s32[640]{0:T(1024)S(1)}, s32[640]{0:T(1024)}, u32[]{:S(2)}) copy-start(s32[640]{0:T(1024)} %param.7) | copy-start | bytes 7684
Sparse Core Ops, SparseCore 0:
  10.5 58.1 all-gather.5
  70.5 210.3 all-gather.3
where the time goes:
time: 343 us; the launch traced here: 342 us
  waiting for transfers between devices  265 us (77%)
  blocking collectives  27.4 us (8%)
  matrix products  18.6 us (5%)
  between operations  16.7 us (5%)
  local copies, waits for them, and re-layouts  9.13 us (3%)
  other arithmetic  5.29 us (2%)
    all_gather x1, waiting for transfers between devices, shards(): weight_full = lax.all_gather(out_weight, 'dp', axis=0, tiled=True)  204 us
    all_gather x1, waiting for transfers between devices, shards(): gathered = lax.all_gather(hidden, 'vocab', axis=0, tiled=True)  59.4 us
    all_to_all x2, blocking collectives, from_everyone(): lax.all_to_all(jnp.broadcast_to(x[None], (devices, *x.shape)), axis, 0, 0...  27.4 us
    dot_general x1, matrix products, shards(): logits = jnp.dot(gathered, weight_full, preferred_element_type=jnp.float32)  18.6 us
    unnamed x4, local copies, waits for them, and re-layouts  7.78 us
  transfers between devices with their start and end apart: 2, of which 2 were waited for; matrix products, arithmetic and copies ran while one was open for 2% of the time, Pallas kernels for 0%

commit v1 on v0

--- a/solution.py
+++ b/solution.py
@@ -56,7 +56,21 @@
     gathered = lax.all_gather(hidden, "vocab", axis=0, tiled=True)
     width_here = out_weight.shape[1]
     first_column = lax.axis_index("vocab") * width_here
-    weight_full = lax.all_gather(out_weight, "dp", axis=0, tiled=True)
+    ways, here, turn = (lax.axis_size("dp"), lax.axis_index("dp"), out_weight.shape[0])
+    shape = [n * ways if d == 0 else n for d, n in enumerate(out_weight.shape)]
+    full = lax.dynamic_update_slice_in_dim(
+        jnp.zeros(shape, out_weight.dtype), out_weight, here * turn, axis=0
+    )
+    going_up = going_down = out_weight
+    for far in range(1, ways // 2 + 1):
+        going_up = lax.ppermute(going_up, "dp", [(d, (d + 1) % ways) for d in range(ways)])
+        full = lax.dynamic_update_slice_in_dim(full, going_up, (here - far) % ways * turn, axis=0)
+        if 2 * far < ways:
+            going_down = lax.ppermute(going_down, "dp", [(d, (d - 1) % ways) for d in range(ways)])
+            full = lax.dynamic_update_slice_in_dim(
+                full, going_down, (here + far) % ways * turn, axis=0
+            )
+    weight_full = full
     logits = jnp.dot(gathered, weight_full, preferred_element_type=jnp.float32)
     columns = jnp.arange(width_here, dtype=jnp.int32)
     local_targets = labels - first_column

time: 343 us -> 315 us (0.918)
  waiting for transfers between devices: 265 us -> 189 us
  local copies, waits for them, and re-layouts: 9.13 us -> 38.6 us
  starting transfers between devices: 0.08 us -> 13.5 us
  blocking collectives: 27.4 us -> 31 us
    all_gather x1 -> x0, waiting for transfers between devices: 204 us -> none  [shards(): weight_full = lax.all_gather(out_weight, 'dp', axis=0, tiled=True)]
    ppermute x0 -> x7, waiting for transfers between devices: none -> 189 us  [the longest x4 189 us: shards(): lax.ppermute(going_up, 'dp', [(d, (d + 1) % ways) for d in range(ways)])]
    all_gather x1, waiting for transfers between devices: 59.4 us -> 0.01 us  [shards(): gathered = lax.all_gather(hidden, 'vocab', axis=0, tiled=True)]
    dynamic_update_slice x0 -> x8, local copies, waits for them, and re-layouts: none -> 22.1 us  [the longest x4 11.8 us: shards(): lax.dynamic_update_slice_in_dim(full, going_up, (here - far) % ways * tur...]
    ppermute x0 -> x7, starting transfers between devices: none -> 13.4 us  [the longest x3 10.9 us: shards(): lax.ppermute(going_down, 'dp', [(d, (d - 1) % ways) for d in range(ways)])]
    broadcast_in_dim x0 -> x1, local copies, waits for them, and re-layouts: none -> 7.31 us  [shards(): jnp.zeros(shape, out_weight.dtype)]
    all_to_all x2, blocking collectives: 27.4 us -> 31 us  [from_everyone(): lax.all_to_all(jnp.broadcast_to(x[None], (devices, *x.shape)), axis, 0, 0...]
    unnamed x4 -> x8, local copies, waits for them, and re-layouts: 7.78 us -> 7.84 us
  transfers between devices with their start and end apart: 2 -> 8, of which waited for: 2 -> 4; matrix products, arithmetic and copies ran while one was open for 2% -> 11% of each run, Pallas kernels for 0% -> 0%
where the time goes in v1:
time: 315 us
  waiting for transfers between devices  189 us (60%)
  local copies, waits for them, and re-layouts  38.6 us (12%)
  blocking collectives  31 us (10%)
  matrix products  21.2 us (7%)
  between operations  16.6 us (5%)
  starting transfers between devices  13.5 us (4%)
  other arithmetic  4.6 us (1%)
    ppermute x4, waiting for transfers between devices, shards(): lax.ppermute(going_up, 'dp', [(d, (d + 1) % ways) for d in range(ways)])  189 us
    all_to_all x2, blocking collectives, from_everyone(): lax.all_to_all(jnp.broadcast_to(x[None], (devices, *x.shape)), axis, 0, 0...  31 us
    dot_general x1, matrix products, shards(): logits = jnp.dot(gathered, weight_full, preferred_element_type=jnp.float32)  21.2 us
    dynamic_update_slice x4, local copies, waits for them, and re-layouts, shards(): lax.dynamic_update_slice_in_dim(full, going_up, (here - far) % ways * tur...  11.8 us
    ppermute x3, starting transfers between devices, shards(): lax.ppermute(going_down, 'dp', [(d, (d - 1) % ways) for d in range(ways)])  10.9 us
    dynamic_update_slice x3, local copies, waits for them, and re-layouts, shards(): lax.dynamic_update_slice_in_dim(full, going_down, (here + far) % ways * t...  8.56 us
    unnamed x8, local copies, waits for them, and re-layouts  7.84 us
    broadcast_in_dim x1, local copies, waits for them, and re-layouts, shards(): jnp.zeros(shape, out_weight.dtype)  7.31 us
  transfers between devices with their start and end apart: 8, of which 4 were waited for; matrix products, arithmetic and copies ran while one was open for 11% of the time, Pallas kernels for 0%

profile of v1, /device:TPU:1, one launch (start us, length us, event | category | flops | bytes accessed | tf_op | source)
XLA Modules:
  0.0 314.8 jit_solution(821959312679322440)
XLA Ops:
  7.2 0.0 all-gather.3.cloned.1.call-start
  7.2 2.5 collective-permute-start
  9.7 0.0 all-gather.3.cloned.1.call-update
  9.8 4.6 %collective-permute-start.1 = (bf16[512,2560]{1,0:T(8,128)(2,1)}, bf16[512,2560]{1,0:T(8,128)(2,1)}, u32[]{:S(2)}, u32[]{:S(2)}) collective-permute-start(bf16[512,2560]{1,0:T(8,128)(2,1)} %param.5), channel_id=1, source_target_pairs={{0,224},{32,0},{64,32},{96,64},{128,96},{160,128},{192,160},{224,1... | collective-permute-start | bytes 7864328 | tf_op jit(solution)/shard_map/ppermute | solution.py:69
  14.4 56.1 %collective-permute-done = bf16[512,2560]{1,0:T(8,128)(2,1)S(1)} collective-permute-done((bf16[512,2560]{1,0:T(8,128)(2,1)}, bf16[512,2560]{1,0:T(8,128)(2,1)S(1)}, u32[]{:S(2)}, u32[]{:S(2)}) %collective-permute-start) | collective-permute-done | bytes 2621472 | tf_op jit(solution)/shard_map/ppermute | solution.py:66
  70.5 0.0 collective-permute-start.2
  70.5 0.0 collective-permute-done.1
  70.5 3.2 %collective-permute-start.3 = (bf16[512,2560]{1,0:T(8,128)(2,1)}, bf16[512,2560]{1,0:T(8,128)(2,1)}, u32[]{:S(2)}, u32[]{:S(2)}) collective-permute-start(bf16[512,2560]{1,0:T(8,128)(2,1)} %collective-permute-done.1), channel_id=1, source_target_pairs={{0,224},{32,0},{64,32},{96,64},{128,96},{160,128},{192,160},{224,1... | collective-permute-start | bytes 7864328 | tf_op jit(solution)/shard_map/ppermute | solution.py:69
  73.6 55.3 %collective-permute-done.2 = bf16[512,2560]{1,0:T(8,128)(2,1)} collective-permute-done((bf16[512,2560]{1,0:T(8,128)(2,1)S(1)}, bf16[512,2560]{1,0:T(8,128)(2,1)}, u32[]{:S(2)}, u32[]{:S(2)}) %collective-permute-start.2) | collective-permute-done | bytes 2621472 | tf_op jit(solution)/shard_map/ppermute | solution.py:66
  128.9 0.0 collective-permute-start.4
  129.0 0.0 copy-start
  129.0 0.0 copy-start.1
  129.0 0.0 collective-permute-done.3
  129.0 3.1 collective-permute-start.5
  132.1 7.3 %broadcast_in_dim.10 = bf16[4096,2560]{1,0:T(8,128)(2,1)} broadcast(bf16[]{:T(256)} %constant.57.clone.1), dimensions={} | broadcast | bytes 20971522 | tf_op jit(solution)/shard_map/broadcast_in_dim | solution.py:62
  139.4 0.0 copy-done
  139.4 1.7 constant_dynamic-update-slice_fusion.7
  141.1 45.7 %collective-permute-done.4 = bf16[512,2560]{1,0:T(8,128)(2,1)} collective-permute-done((bf16[512,2560]{1,0:T(8,128)(2,1)}, bf16[512,2560]{1,0:T(8,128)(2,1)}, u32[]{:S(2)}, u32[]{:S(2)}) %collective-permute-start.4) | collective-permute-done | bytes 2621472 | tf_op jit(solution)/shard_map/ppermute | solution.py:66
  186.8 0.0 collective-permute-start.6
  186.8 0.0 copy-done.1
  186.8 1.6 constant_dynamic-update-slice_fusion.6
  188.4 3.4 %constant_dynamic-update-slice_fusion.5 = bf16[4096,2560]{1,0:T(8,128)(2,1)} fusion(bf16[4096,2560]{1,0:T(8,128)(2,1)} %constant_dynamic-update-slice_fusion.6, bf16[512,2560]{1,0:T(8,128)(2,1)} %collective-permute-done.1, s32[]{:T(128)S(6)} %select_n.63), kind=kLoop, calls=%fused_computation.30 | loop fusion | bytes 5242884 | tf_op jit(solution)/shard_map/dynamic_update_slice | solution.py:70
  191.9 3.4 %constant_dynamic-update-slice_fusion.4 = bf16[4096,2560]{1,0:T(8,128)(2,1)} fusion(bf16[4096,2560]{1,0:T(8,128)(2,1)} %constant_dynamic-update-slice_fusion.5, bf16[512,2560]{1,0:T(8,128)(2,1)} %collective-permute-done.2, s32[]{:T(128)S(6)} %select_n.65), kind=kLoop, calls=%fused_computation.29 | loop fusion | bytes 5242884 | tf_op jit(solution)/shard_map/dynamic_update_slice | solution.py:67
  195.3 3.4 %constant_dynamic-update-slice_fusion.3 = bf16[4096,2560]{1,0:T(8,128)(2,1)} fusion(bf16[4096,2560]{1,0:T(8,128)(2,1)} %constant_dynamic-update-slice_fusion.4, bf16[512,2560]{1,0:T(8,128)(2,1)} %collective-permute-done.3, s32[]{:T(128)S(6)} %select_n.67), kind=kLoop, calls=%fused_computation.28 | loop fusion | bytes 5242884 | tf_op jit(solution)/shard_map/dynamic_update_slice | solution.py:70
  198.7 3.4 %constant_dynamic-update-slice_fusion.2 = bf16[4096,2560]{1,0:T(8,128)(2,1)} fusion(bf16[4096,2560]{1,0:T(8,128)(2,1)} %constant_dynamic-update-slice_fusion.3, bf16[512,2560]{1,0:T(8,128)(2,1)} %collective-permute-done.4, s32[]{:T(128)S(6)} %select_n.69), kind=kLoop, calls=%fused_computation.27 | loop fusion | bytes 5242884 | tf_op jit(solution)/shard_map/dynamic_update_slice | solution.py:67
  202.1 0.0 collective-permute-done.5
  202.1 1.7 constant_dynamic-update-slice_fusion.1
  203.8 0.0 all-gather.3.cloned.1.call-done
  203.8 7.8 %reshape.54 = bf16[640,4096]{1,0:T(8,128)(2,1)} reshape(bf16[32,20,4096]{2,1,0:T(8,128)(2,1)} %all-gather.3.cloned.1.call-done) | data formatting | bytes 10485760
  211.6 32.2 %collective-permute-done.6 = bf16[512,2560]{1,0:T(8,128)(2,1)} collective-permute-done((bf16[512,2560]{1,0:T(8,128)(2,1)}, bf16[512,2560]{1,0:T(8,128)(2,1)}, u32[]{:S(2)}, u32[]{:S(2)}) %collective-permute-start.6) | collective-permute-done | bytes 2621472 | tf_op jit(solution)/shard_map/ppermute | solution.py:66
  243.8 3.4 %constant_dynamic-update-slice_fusion = bf16[4096,2560]{1,0:T(8,128)(2,1)} fusion(bf16[4096,2560]{1,0:T(8,128)(2,1)} %constant_dynamic-update-slice_fusion.1, bf16[512,2560]{1,0:T(8,128)(2,1)} %collective-permute-done.6, s32[]{:T(128)S(6)} %select_n.73), kind=kLoop, calls=%fused_computation.25 | loop fusion | bytes 5242884 | tf_op jit(solution)/shard_map/dynamic_update_slice | solution.py:67
  247.2 21.2 %fusion.10 = (f32[640]{0:T(1024)S(1)}, f32[2560,640]{1,0:T(8,128)S(1)}) fusion(bf16[4096,2560]{1,0:T(8,128)(2,1)} %constant_dynamic-update-slice_fusion, bf16[640,4096]{1,0:T(8,128)(2,1)} %reshape.54), kind=kOutput, calls=%fused_computation.37 | convolution fusion | flops 13423410176 | bytes 32770560 | tf_op jit(solution)/shard_map/dot_general | solution.py:74
  268.4 0.0 copy-start.2
  268.4 1.8 fusion.1
  270.3 20.2 %all_to_all.11 = f32[32,3,640]{2,1,0:T(4,128)S(1)} all-to-all(f32[32,3,640]{2,1,0:T(4,128)S(1)} %broadcast_in_dim.12), channel_id=1, replica_groups=mesh['dp'=8,'vocab'=32] {'vocab'}, dimensions={0} | all-to-all | bytes 491520 | tf_op jit(solution)/shard_map/all_to_all | solution.py:9
  290.5 0.2 fusion.8
  291.5 0.0 copy-done.2
  291.5 1.3 fusion.7
  292.8 1.4 pad_maximum_fusion.1
  294.1 10.8 %all_to_all.12 = f32[8,1,2]{2,1,0:T(1,128)S(1)} all-to-all(f32[8,1,2]{2,1,0:T(1,128)S(1)} %broadcast_in_dim.13), channel_id=1, replica_groups=mesh['dp'=8,'vocab'=32] {'dp'}, dimensions={0} | all-to-all | bytes 128 | tf_op jit(solution)/shard_map/all_to_all | solution.py:9
  304.9 0.6 fusion.9
  (43 shorter events, 0.8 us)
Async XLA Ops:
  7.2 196.6 %all-gather.3.cloned.1.call-start = ((), (), s32[]{:S(2)}) async-start(), calls=%async_computation.2 | async-start | bytes 6488064 | tf_op jit(solution)/shard_map/all_gather | solution.py:56
  7.2 63.2 %collective-permute-start = (bf16[512,2560]{1,0:T(8,128)(2,1)}, bf16[512,2560]{1,0:T(8,128)(2,1)S(1)}, u32[]{:S(2)}, u32[]{:S(2)}) collective-permute-start(bf16[512,2560]{1,0:T(8,128)(2,1)} %param.5), channel_id=1, source_target_pairs={{0,32},{32,64},{64,96},{96,128},{128,160},{160,192},{192,224},{224... | collective-permute-start | bytes 7864328 | tf_op jit(solution)/shard_map/ppermute | solution.py:66
  9.8 60.7 %collective-permute-start.1 = (bf16[512,2560]{1,0:T(8,128)(2,1)}, bf16[512,2560]{1,0:T(8,128)(2,1)}, u32[]{:S(2)}, u32[]{:S(2)}) collective-permute-start(bf16[512,2560]{1,0:T(8,128)(2,1)} %param.5), channel_id=1, source_target_pairs={{0,224},{32,0},{64,32},{96,64},{128,96},{160,128},{192,160},{224,1... | collective-permute-start | bytes 7864328 | tf_op jit(solution)/shard_map/ppermute | solution.py:69
  70.5 58.5 %collective-permute-start.2 = (bf16[512,2560]{1,0:T(8,128)(2,1)S(1)}, bf16[512,2560]{1,0:T(8,128)(2,1)}, u32[]{:S(2)}, u32[]{:S(2)}) collective-permute-start(bf16[512,2560]{1,0:T(8,128)(2,1)S(1)} %collective-permute-done), channel_id=1, source_target_pairs={{0,32},{32,64},{64,96},{96,128},{128,160},{160,192},{192,224},{224... | collective-permute-start | bytes 7864328 | tf_op jit(solution)/shard_map/ppermute | solution.py:66
  70.5 58.5 %collective-permute-start.3 = (bf16[512,2560]{1,0:T(8,128)(2,1)}, bf16[512,2560]{1,0:T(8,128)(2,1)}, u32[]{:S(2)}, u32[]{:S(2)}) collective-permute-start(bf16[512,2560]{1,0:T(8,128)(2,1)} %collective-permute-done.1), channel_id=1, source_target_pairs={{0,224},{32,0},{64,32},{96,64},{128,96},{160,128},{192,160},{224,1... | collective-permute-start | bytes 7864328 | tf_op jit(solution)/shard_map/ppermute | solution.py:69
  128.9 57.8 %collective-permute-start.4 = (bf16[512,2560]{1,0:T(8,128)(2,1)}, bf16[512,2560]{1,0:T(8,128)(2,1)}, u32[]{:S(2)}, u32[]{:S(2)}) collective-permute-start(bf16[512,2560]{1,0:T(8,128)(2,1)} %collective-permute-done.2), channel_id=1, source_target_pairs={{0,32},{32,64},{64,96},{96,128},{128,160},{160,192},{192,224},{224... | collective-permute-start | bytes 7864328 | tf_op jit(solution)/shard_map/ppermute | solution.py:66
  129.0 10.4 %copy-start = (bf16[512,2560]{1,0:T(8,128)(2,1)S(1)}, bf16[512,2560]{1,0:T(8,128)(2,1)}, u32[]{:S(2)}) copy-start(bf16[512,2560]{1,0:T(8,128)(2,1)} %param.5) | copy-start | bytes 7864324
  129.0 57.8 %copy-start.1 = (s32[640]{0:T(1024)S(1)}, s32[640]{0:T(1024)}, u32[]{:S(2)}) copy-start(s32[640]{0:T(1024)} %param.6) | copy-start | bytes 7684
  129.0 73.1 %collective-permute-start.5 = (bf16[512,2560]{1,0:T(8,128)(2,1)}, bf16[512,2560]{1,0:T(8,128)(2,1)S(1)}, u32[]{:S(2)}, u32[]{:S(2)}) collective-permute-start(bf16[512,2560]{1,0:T(8,128)(2,1)} %collective-permute-done.3), channel_id=1, source_target_pairs={{0,224},{32,0},{64,32},{96,64},{128,96},{160,128},{192,160},{224,1... | collective-permute-start | bytes 7864328 | tf_op jit(solution)/shard_map/ppermute | solution.py:69
  186.8 57.0 %collective-permute-start.6 = (bf16[512,2560]{1,0:T(8,128)(2,1)}, bf16[512,2560]{1,0:T(8,128)(2,1)}, u32[]{:S(2)}, u32[]{:S(2)}) collective-permute-start(bf16[512,2560]{1,0:T(8,128)(2,1)} %collective-permute-done.4), channel_id=1, source_target_pairs={{0,32},{32,64},{64,96},{96,128},{128,160},{160,192},{192,224},{224... | collective-permute-start | bytes 7864328 | tf_op jit(solution)/shard_map/ppermute | solution.py:66
  268.4 23.1 %copy-start.2 = (s32[640]{0:T(1024)S(1)}, s32[640]{0:T(1024)}, u32[]{:S(2)}) copy-start(s32[640]{0:T(1024)} %param.7) | copy-start | bytes 7684
Sparse Core Ops, SparseCore 0:
  10.5 58.1 all-gather.2
